TPU v7x, 128 devices: a whole 4x4x4 slice. The times are simulated.
128 devices in a mesh: pipe: 4 (over y), dp: 32 (over z, x, core).
Axes of the slice: x: 4, y: 4, z: 4, core: 2. Of those that a mesh axis runs over, the one named last changes fastest.
Arguments:
- x_in: bfloat16 [4, 1024, 4096], P(None, 'dp'), may hold values from -6 to 6
- cotangent: bfloat16 [4, 1024, 4096], P(None, 'dp'), may hold values from -6 to 6
- weights: bfloat16 [4, 64, 64, 2048], P('pipe', 'dp'), as said below
- live_rows: int32 [4, 64, 32], P('pipe'), may hold values from 0 to 63, as said below
- moment: float32 [4, 64, 64, 2048], P('pipe', 'dp'), may hold values from -0.125 to 0.125
- second: float32 [4, 64, 64, 2048], P('pipe', 'dp'), may hold values from 1.2207031e-05 to 0.00024414062
Outputs:
- weights_out: bfloat16 [4, 64, 64, 2048], P('pipe', 'dp')
- moment_out: float32 [4, 64, 64, 2048], P('pipe', 'dp')
- second_out: float32 [4, 64, 64, 2048], P('pipe', 'dp')
Inputs may be any that keep to these rules, and one draw needn't show every extreme that they name: `live_rows`: for each layer and block column the 32 entries are distinct block rows. `weights`: entry [l, j, b, k * 64 + a] is the weight from input feature live_rows[l, j, k] * 64 + a to output feature j * 64 + b; unstored blocks are zero.
All inputs are finite; a program needn't handle non-finite values.
Results may differ from a plain program's by a relative error of at most 0.009.
Values may be sent and summed in bfloat16 or wider, within the bound.
A program may use at most 256 MiB of HBM per device.

v0:
```python
import math
import jax
import jax.numpy as jnp
from jax import lax
from jax.sharding import PartitionSpec as P

HEAD = 128
column_group = 8


def shifted(value, axis, steps):
    count = lax.axis_size(axis)
    leading, last = (max(0, -steps), min(count, count - steps))
    return lax.ppermute(value, axis, [(source, source + steps) for source in range(leading, last)])


def shrink(magnitude, threshold):
    return jnp.maximum(magnitude - threshold, 0.0) / jnp.maximum(magnitude, threshold)


def column_products(normed, section_weights, live_index):
    tokens, features = normed.shape
    column_count, block_size, wide = section_weights.shape
    live_count = live_index.shape[1]
    group_count = column_count // column_group
    normed_blocks = normed.reshape(tokens, column_count, block_size)

    def column_per_group(members):
        weight_part, index_part = members
        picked = jnp.take(normed_blocks, index_part.reshape(-1), axis=1).reshape(
            tokens, column_group, wide
        )
        return jnp.einsum("tjk,jbk->tjb", picked, weight_part, preferred_element_type=jnp.float32)

    result = lax.map(
        column_per_group,
        (
            section_weights.reshape(group_count, column_group, block_size, wide),
            live_index.reshape(group_count, column_group, live_count),
        ),
    )
    return result.transpose(1, 0, 2, 3).reshape(tokens, features)


def dense_transposed(section_weights, live_index):
    column_count, block_size, wide = section_weights.shape
    live_count = live_index.shape[1]
    group_count = column_count // column_group
    features = column_count * block_size
    targets = jnp.arange(column_count, dtype=jnp.int32)

    def dense_per_group(members):
        weight_part, index_part = members
        chosen = (index_part[:, :, None] == targets[None, None, :]).astype(jnp.bfloat16)
        slab = jnp.einsum(
            "jkr,jbka->jbra",
            chosen,
            weight_part.reshape(column_group, block_size, live_count, block_size),
            preferred_element_type=jnp.float32,
        )
        return slab.astype(jnp.bfloat16).reshape(column_group * block_size, features)

    slabs = lax.map(
        dense_per_group,
        (
            section_weights.reshape(group_count, column_group, block_size, wide),
            live_index.reshape(group_count, column_group, live_count),
        ),
    )
    return slabs.reshape(features, features)


def layer_forward(entering, section_weights, live_index):
    as_float = entering.astype(jnp.float32)
    inverse_rms = lax.rsqrt(jnp.mean(as_float * as_float, axis=-1, keepdims=True) + 1e-05)
    normed = (as_float * inverse_rms).astype(jnp.bfloat16)
    pre_act = column_products(normed, section_weights, live_index)
    return ((as_float + jax.nn.silu(pre_act)).astype(jnp.bfloat16), normed, pre_act)


def layer_backward(arriving, entering, pre_act, dense_weights):
    as_float = entering.astype(jnp.float32)
    inverse_rms = lax.rsqrt(jnp.mean(as_float * as_float, axis=-1, keepdims=True) + 1e-05)
    sigmoid_z = jax.nn.sigmoid(pre_act)
    grad_pre = (
        arriving.astype(jnp.float32) * (sigmoid_z * (1.0 + pre_act * (1.0 - sigmoid_z)))
    ).astype(jnp.bfloat16)
    grad_normed = jnp.dot(grad_pre, dense_weights, preferred_element_type=jnp.float32)
    scaled = as_float * inverse_rms
    leaving = (
        arriving.astype(jnp.float32)
        + inverse_rms
        * (grad_normed - scaled * jnp.mean(grad_normed * scaled, axis=-1, keepdims=True))
    ).astype(jnp.bfloat16)
    return (leaving, grad_pre)


def local(x_in, cotangent, weights, live_rows, moment, second):
    sections = lax.axis_size("pipe")
    section_index = lax.axis_index("pipe")
    micro_count, tokens, features = x_in.shape
    column_count = live_rows.shape[1]
    live_count = live_rows.shape[2]
    own_columns = weights.shape[1]
    block_size = weights.shape[2]
    live_index = live_rows[0]
    section_weights = lax.all_gather(weights[0], "dp", axis=0, tiled=True)
    tick_count = micro_count + sections - 1
    incoming = jnp.zeros((tokens, features), jnp.bfloat16)
    saved_in = jnp.zeros((micro_count, tokens, features), jnp.bfloat16)
    saved_normed = jnp.zeros((micro_count, tokens, features), jnp.bfloat16)
    saved_pre = jnp.zeros((micro_count, tokens, features), jnp.float32)
    for tick_index in range(tick_count):
        slot_raw = tick_index - section_index
        active_now = (slot_raw >= 0) & (slot_raw < micro_count)
        slot_index = jnp.clip(slot_raw, 0, micro_count - 1)
        entering = jnp.where(section_index == 0, x_in[min(tick_index, micro_count - 1)], incoming)

        def forward_work(state, slot_index=slot_index):
            current, store_in, store_normed, store_pre = state
            outgoing, normed, pre_act = layer_forward(current, section_weights, live_index)
            return (
                outgoing,
                store_in.at[slot_index].set(current),
                store_normed.at[slot_index].set(normed),
                store_pre.at[slot_index].set(pre_act),
            )

        def forward_skip(state):
            current, store_in, store_normed, store_pre = state
            return (jnp.zeros_like(current), store_in, store_normed, store_pre)

        outgoing, saved_in, saved_normed, saved_pre = lax.cond(
            active_now, forward_work, forward_skip, (entering, saved_in, saved_normed, saved_pre)
        )
        if tick_index + 1 < tick_count:
            incoming = shifted(outgoing, "pipe", 1)
    dense_weights = dense_transposed(section_weights, live_index)
    incoming_grad = jnp.zeros((tokens, features), jnp.bfloat16)
    saved_grad = jnp.zeros((micro_count, tokens, features), jnp.bfloat16)
    for tick_index in range(tick_count):
        slot_raw = tick_index - (sections - 1 - section_index)
        active_now = (slot_raw >= 0) & (slot_raw < micro_count)
        slot_index = jnp.clip(slot_raw, 0, micro_count - 1)
        arriving = jnp.where(
            section_index == sections - 1,
            cotangent[min(tick_index, micro_count - 1)],
            incoming_grad,
        )

        def backward_work(state, slot_index=slot_index):
            current, store_grad = state
            leaving, grad_pre = layer_backward(
                current, saved_in[slot_index], saved_pre[slot_index], dense_weights
            )
            return (leaving, store_grad.at[slot_index].set(grad_pre))

        def backward_skip(state):
            current, store_grad = state
            return (jnp.zeros_like(current), store_grad)

        leaving, saved_grad = lax.cond(
            active_now, backward_work, backward_skip, (arriving, saved_grad)
        )
        if tick_index + 1 < tick_count:
            incoming_grad = shifted(leaving, "pipe", -1)
    all_rows = micro_count * tokens
    normed_blocks = saved_normed.reshape(all_rows, column_count, block_size)
    grad_blocks = saved_grad.reshape(all_rows, column_count, block_size)
    inverse_tokens = 1.0 / (all_rows * lax.axis_size("dp"))
    cast_type = jnp.bfloat16
    group_size = math.gcd(column_count, column_group)
    group_count = column_count // group_size
    index_part = live_index.reshape(group_count, group_size, live_count)
    grad_part = grad_blocks.reshape(all_rows, group_count, group_size, block_size).transpose(
        1, 0, 2, 3
    )

    def grad_per_group(members):
        index_group, grad_group = members
        picked = jnp.take(normed_blocks, index_group.reshape(-1), axis=1).reshape(
            all_rows, group_size, live_count * block_size
        )
        return (
            jnp.einsum("tjk,tjb->jbk", picked, grad_group, preferred_element_type=jnp.float32)
            * inverse_tokens
        ).astype(cast_type)

    gradient = lax.psum_scatter(
        lax.map(grad_per_group, (index_part, grad_part)).reshape(
            column_count, block_size, live_count * block_size
        ),
        "dp",
        scatter_dimension=0,
        tiled=True,
    ).astype(jnp.float32)
    rate = 0.1 / math.sqrt(live_count * block_size)
    moment_new = 0.9 * moment[0] + 0.1 * gradient
    second_new = 0.95 * second[0] + 0.05 * gradient * gradient
    stepped = weights[0].astype(jnp.float32) - rate * moment_new / (jnp.sqrt(second_new) + 1e-08)
    own_index = lax.dynamic_slice_in_dim(
        live_index, lax.axis_index("dp") * own_columns, own_columns, 0
    )
    blocked = stepped.reshape(own_columns, block_size, live_count, block_size)
    magnitude = jnp.sqrt(jnp.sum(blocked * blocked, axis=(1, 3)))
    leafed = (
        blocked * shrink(magnitude, 0.15 * math.sqrt(block_size / live_count))[:, None, :, None]
    )
    block_squares = jnp.sum(leafed * leafed, axis=(1, 3))
    head_count = features // HEAD
    head_index = own_index // (HEAD // block_size)
    onehot = (
        head_index[:, :, None] == jnp.arange(head_count, dtype=jnp.int32)[None, None, :]
    ).astype(jnp.float32)
    head_squares = lax.psum(jnp.sum(onehot * block_squares[:, :, None], axis=(0, 1)), "dp")
    head_factor = shrink(jnp.sqrt(head_squares), 0.45 * math.sqrt(HEAD))
    headed = leafed * jnp.sum(onehot * head_factor[None, None, :], axis=2)[:, None, :, None]
    layer_squares = lax.psum(jnp.sum(headed * headed), "dp")
    layer_factor = shrink(jnp.sqrt(layer_squares), 0.45 * math.sqrt(features))
    weights_out = (
        (headed * layer_factor)
        .astype(jnp.bfloat16)
        .reshape(own_columns, block_size, live_count * block_size)
    )
    return (weights_out[None], moment_new[None], second_new[None])


def solution(mesh):
    placed = (
        P(None, "dp", None),
        P(None, "dp", None),
        P("pipe", "dp", None, None),
        P("pipe", None, None),
        P("pipe", "dp", None, None),
        P("pipe", "dp", None, None),
    )
    return jax.shard_map(
        local,
        mesh=mesh,
        in_specs=placed,
        out_specs=(
            P("pipe", "dp", None, None),
            P("pipe", "dp", None, None),
            P("pipe", "dp", None, None),
        ),
        check_vma=False,
    )
```

profile of v0, /device:TPU:1, one launch (start us, length us, event | category | flops | bytes accessed | tf_op | source)
XLA Modules:
  0.0 1587.1 jit_solution(2375558503213230283)
XLA Ops:
  8.0 78.6 %all-gather.3.cloned.1.call-done = bf16[1,64,64,2048]{3,2,0,1:T(8,128)(2,1)} async-done(((bf16[1,2,64,2048]{3,2,0,1:T(8,128)(2,1)}), bf16[1,64,64,2048]{3,2,0,1:T(8,128)(2,1)}) %all-gather.3.cloned.1.call-update) | async-done | bytes 16777232 | tf_op jit(solution)/shard_map/all_gather | solution.py:107
  87.3 84.7 %conditional.14 = (bf16[32,4096]{1,0:T(8,128)(2,1)S(1)}, bf16[4,32,4096]{2,1,0:T(8,128)(2,1)}, bf16[4,32,4096]{2,1,0:T(8,128)(2,1)}, f32[4,32,4096]{2,1,0:T(8,128)}) conditional(s32[]{:T(128)} %convert_element_type.242, () %tuple.272, (bf16[4,32,4096]{2,1,0:T(8,128)(2,1)}, pred[32,4096]{1,0:T(8,128)(4,1)S(1)}, bf16[32,4096]{1,0:T(8,128)(2,1)S(1)}, ...), branch_computations={%region_0.1_spmd, %region_1.7_spmd} | conditional | flops 69864752 | bytes 28641040 | solution.py:133
  95.7 69.9 %while.112 = (s32[]{:T(128)}, f32[8,32,8,64]{3,1,2,0:T(8,128)}, bf16[8,8,64,2048]{3,2,1,0:T(8,128)(2,1)}, s32[8,8,32]{2,1,0:T(8,128)S(1)}, bf16[32,64,64]{2,0,1:T(8,128)(2,1)S(1)}, /*index=5*/s32[]{:T(128)}) while((s32[]{:T(128)}, f32[8,32,8,64]{3,1,2,0:T(8,128)}, bf16[8,8,64,2048]{3,2,1,0:T(8,128)(2,1)}, s32[8,8,32]{2,1,0:T(8,128)S(1)}, ...), condition=%wide.region_4.5_spmd, body=%wide.region_3.4_spmd.sunk | while | flops 67636480 | bytes 11680329 | solution.py:35
  180.1 83.5 %conditional.15 = (bf16[32,4096]{1,0:T(8,128)(2,1)}, bf16[4,32,4096]{2,1,0:T(8,128)(2,1)}, bf16[4,32,4096]{2,1,0:T(8,128)(2,1)}, f32[4,32,4096]{2,1,0:T(8,128)}) conditional(s32[]{:T(128)} %convert_element_type.241, (bf16[4,32,4096]{2,1,0:T(8,128)(2,1)}, bf16[4,32,4096]{2,1,0:T(8,128)(2,1)}, f32[4,32,4096]{2,1,0:T(8,128)}) %tuple.274, ...), branch_computations={%region_6.8_spmd, %region_7.13_spmd} | conditional | flops 69864752 | bytes 21301482 | solution.py:133
  187.9 69.8 %while.113 = (s32[]{:T(128)}, f32[8,32,8,64]{3,1,2,0:T(8,128)}, bf16[8,8,64,2048]{3,2,1,0:T(8,128)(2,1)}, s32[8,8,32]{2,1,0:T(8,128)S(1)}, bf16[32,64,64]{2,0,1:T(8,128)(2,1)S(1)}, /*index=5*/s32[]{:T(128)}) while((s32[]{:T(128)}, f32[8,32,8,64]{3,1,2,0:T(8,128)}, bf16[8,8,64,2048]{3,2,1,0:T(8,128)(2,1)}, s32[8,8,32]{2,1,0:T(8,128)S(1)}, ...), condition=%wide.region_10.11_spmd, body=%wide.region_9.10_spmd.sunk | while | flops 67636480 | bytes 11680329 | solution.py:35
  272.8 83.2 %conditional.16 = (bf16[32,4096]{1,0:T(8,128)(2,1)}, bf16[4,32,4096]{2,1,0:T(8,128)(2,1)}, bf16[4,32,4096]{2,1,0:T(8,128)(2,1)}, f32[4,32,4096]{2,1,0:T(8,128)}) conditional(s32[]{:T(128)} %convert_element_type.240, (bf16[4,32,4096]{2,1,0:T(8,128)(2,1)}, bf16[4,32,4096]{2,1,0:T(8,128)(2,1)}, f32[4,32,4096]{2,1,0:T(8,128)}) %tuple.276, ...), branch_computations={%region_12.14_spmd, %region_13.19_spmd} | conditional | flops 69864752 | bytes 21301482 | solution.py:133
  280.3 69.8 %while.114 = (s32[]{:T(128)}, f32[8,32,8,64]{3,1,2,0:T(8,128)}, bf16[8,8,64,2048]{3,2,1,0:T(8,128)(2,1)}, s32[8,8,32]{2,1,0:T(8,128)S(1)}, bf16[32,64,64]{2,0,1:T(8,128)(2,1)S(1)}, /*index=5*/s32[]{:T(128)}) while((s32[]{:T(128)}, f32[8,32,8,64]{3,1,2,0:T(8,128)}, bf16[8,8,64,2048]{3,2,1,0:T(8,128)(2,1)}, s32[8,8,32]{2,1,0:T(8,128)S(1)}, ...), condition=%wide.region_16.17_spmd, body=%wide.region_15.16_spmd.sunk | while | flops 67636480 | bytes 11680329 | solution.py:35
  364.2 83.4 %conditional.17 = (bf16[32,4096]{1,0:T(8,128)(2,1)}, bf16[4,32,4096]{2,1,0:T(8,128)(2,1)}, bf16[4,32,4096]{2,1,0:T(8,128)(2,1)}, f32[4,32,4096]{2,1,0:T(8,128)}) conditional(s32[]{:T(128)} %convert_element_type.239, (bf16[4,32,4096]{2,1,0:T(8,128)(2,1)}, bf16[4,32,4096]{2,1,0:T(8,128)(2,1)}, f32[4,32,4096]{2,1,0:T(8,128)}) %tuple.278, ...), branch_computations={%region_18.20_spmd, %region_19.25_spmd} | conditional | flops 69864752 | bytes 21301482 | solution.py:133
  371.8 69.8 %while.115 = (s32[]{:T(128)}, f32[8,32,8,64]{3,1,2,0:T(8,128)}, bf16[8,8,64,2048]{3,2,1,0:T(8,128)(2,1)}, s32[8,8,32]{2,1,0:T(8,128)S(1)}, bf16[32,64,64]{2,0,1:T(8,128)(2,1)S(1)}, /*index=5*/s32[]{:T(128)}) while((s32[]{:T(128)}, f32[8,32,8,64]{3,1,2,0:T(8,128)}, bf16[8,8,64,2048]{3,2,1,0:T(8,128)(2,1)}, s32[8,8,32]{2,1,0:T(8,128)S(1)}, ...), condition=%wide.region_22.23_spmd, body=%wide.region_21.22_spmd.sunk | while | flops 67636480 | bytes 11680329 | solution.py:35
  456.2 85.9 %collective-permute-start.4 = (bf16[32,4096]{1,0:T(8,128)(2,1)}, bf16[32,4096]{1,0:T(8,128)(2,1)S(1)}, u32[]{:S(2)}, u32[]{:S(2)}) collective-permute-start(bf16[32,4096]{1,0:T(8,128)(2,1)} %get-tuple-element.1129), channel_id=1, source_target_pairs={{0,32},{32,64},{64,96},{1,33},{33,65},{65,97},{2,34},{34,66},{66,9... | collective-permute-start | bytes 786440 | tf_op jit(solution)/shard_map/ppermute | solution.py:14
  546.9 8.3 collective-permute-start.5
  555.2 356.7 %while.120 = (s32[]{:T(128)}, bf16[8,512,4096]{2,1,0:T(8,128)(2,1)}, bf16[8,8,64,2048]{3,2,1,0:T(8,128)(2,1)}, s32[8,8,32]{2,1,0:T(8,128)}, s32[]{:T(128)}) while((s32[]{:T(128)}, bf16[8,512,4096]{2,1,0:T(8,128)(2,1)}, bf16[8,8,64,2048]{3,2,1,0:T(8,128)(2,1)}, s32[8,8,32]{2,1,0:T(8,128)}, s32[]{:T(128)}) %tuple.546), condition=%wide.region_43.45_spmd.clone, body=%wide.region_42.44_spmd.clone.sunk | while | flops 136331264 | bytes 39849540 | solution.py:63
  562.9 8.2 convert_bitcast_fusion.2
  571.2 11.9 copy.214
  583.1 12.0 broadcast_in_dim.172
  607.5 8.2 convert_bitcast_fusion.2
  615.7 11.9 copy.214
  627.7 12.0 broadcast_in_dim.172
  652.1 8.2 convert_bitcast_fusion.2
  660.3 11.9 copy.214
  672.3 12.0 broadcast_in_dim.172
  696.7 8.2 convert_bitcast_fusion.2
  704.9 11.9 copy.214
  716.9 12.0 broadcast_in_dim.172
  741.3 8.2 convert_bitcast_fusion.2
  749.5 11.9 copy.214
  761.4 12.0 broadcast_in_dim.172
  785.8 8.2 convert_bitcast_fusion.2
  794.0 11.9 copy.214
  806.0 12.0 broadcast_in_dim.172
  830.4 8.2 convert_bitcast_fusion.2
  838.6 11.9 copy.214
  850.6 12.0 broadcast_in_dim.172
  875.0 8.2 convert_bitcast_fusion.2
  883.2 11.9 copy.214
  895.2 12.0 broadcast_in_dim.172
  915.5 83.3 %collective-permute-done.6 = bf16[32,4096]{1,0:T(8,128)(2,1)S(1)} collective-permute-done((bf16[32,4096]{1,0:T(8,128)(2,1)S(1)}, bf16[32,4096]{1,0:T(8,128)(2,1)S(1)}, u32[]{:S(2)}, u32[]{:S(2)}) %collective-permute-start.6) | collective-permute-done | bytes 262176 | tf_op jit(solution)/shard_map/ppermute | solution.py:14
  1009.1 140.8 %collective-permute-done.8 = bf16[32,4096]{1,0:T(8,128)(2,1)S(1)} collective-permute-done((bf16[32,4096]{1,0:T(8,128)(2,1)S(1)}, bf16[32,4096]{1,0:T(8,128)(2,1)S(1)}, u32[]{:S(2)}, u32[]{:S(2)}) %collective-permute-start.8) | collective-permute-done | bytes 262176 | tf_op jit(solution)/shard_map/ppermute | solution.py:14
  1149.9 20.3 %conditional.24 = (bf16[32,4096]{1,0:T(8,128)(2,1)S(1)}, bf16[4,32,4096]{2,1,0:T(8,128)(2,1)}) conditional(s32[]{:T(128)} %convert_element_type.232, bf16[4,32,4096]{2,1,0:T(8,128)(2,1)} %get-tuple-element.1141, (pred[32,4096]{1,0:T(8,128)(4,1)S(1)}, bf16[32,4096]{1,0:T(8,128)(2,1)S(1)}, bf16[32,4096]{1,0:T(8,128)(2,1)S(1)}, s32[]{:T(128)}, ...), branch_computations={%region_59.61_spmd, %region_60.65_spmd} | conditional | flops 1077411840 | bytes 38537416 | solution.py:162
  1155.1 13.9 fusion.45
  1177.3 20.3 %conditional.25 = (bf16[32,4096]{1,0:T(8,128)(2,1)S(1)}, bf16[4,32,4096]{2,1,0:T(8,128)(2,1)}) conditional(s32[]{:T(128)} %convert_element_type.231, bf16[4,32,4096]{2,1,0:T(8,128)(2,1)} %get-tuple-element.1143, (pred[32,4096]{1,0:T(8,128)(4,1)S(1)}, bf16[32,4096]{1,0:T(8,128)(2,1)S(1)}, bf16[32,4096]{1,0:T(8,128)(2,1)S(1)}, s32[]{:T(128)}, ...), branch_computations={%region_64.66_spmd, %region_65.70_spmd} | conditional | flops 1077411840 | bytes 38537416 | solution.py:162
  1182.5 13.9 fusion.59
  1204.7 21.0 %conditional.26 = (bf16[32,4096]{1,0:T(8,128)(2,1)}, bf16[4,32,4096]{2,1,0:T(8,128)(2,1)}) conditional(s32[]{:T(128)} %convert_element_type.230, bf16[4,32,4096]{2,1,0:T(8,128)(2,1)} %get-tuple-element.1145, (pred[32,4096]{1,0:T(8,128)(4,1)S(1)}, bf16[32,4096]{1,0:T(8,128)(2,1)S(1)}, bf16[32,4096]{1,0:T(8,128)(2,1)S(1)}, s32[]{:T(128)}, ...), branch_computations={%region_69.71_spmd, %region_70.75_spmd} | conditional | flops 1077411840 | bytes 38537416 | solution.py:162
  1209.9 13.9 fusion.73
  1243.5 80.6 %while.119 = (s32[]{:T(128)}, bf16[8,8,64,2048]{3,2,1,0:T(8,128)(2,1)}, bf16[8,128,8,64]{1,3,2,0:T(8,128)(2,1)}, s32[8,8,32]{2,1,0:T(8,128)}, bf16[128,64,64]{0,2,1:T(8,128)(2,1)S(1)}, /*index=5*/s32[]{:T(128)}) while((s32[]{:T(128)}, bf16[8,8,64,2048]{3,2,1,0:T(8,128)(2,1)}, bf16[8,128,8,64]{1,3,2,0:T(8,128)(2,1)}, ...), condition=%wide.region_78.80_spmd, body=%wide.region_77.79_spmd.sunk | while | flops 272633088 | bytes 14890569 | solution.py:190
  1324.4 120.4 %reduce-scatter.2.cloned.1.call-done = bf16[2,64,2048]{2,1,0:T(8,128)(2,1)} async-done(((bf16[64,64,2048]{2,1,0:T(8,128)(2,1)}), bf16[2,64,2048]{2,1,0:T(8,128)(2,1)}) %reduce-scatter.2.cloned.1.call-update) | async-done | bytes 524304 | tf_op jit(solution)/shard_map/reduce_scatter | solution.py:189
  1449.1 63.9 %psum.14 = f32[32]{0:T(128)S(1)} all-reduce(f32[32]{0:T(128)S(1)} %select_reduce_fusion.1), channel_id=1, replica_groups=mesh['pipe'=4,'dp'=32] {'dp'}, use_global_device_ids=true, to_apply=%region_85.87 | all-reduce | flops 32 | bytes 256 | tf_op jit(solution)/shard_map/psum | solution.py:215
  1514.2 64.2 %psum.15 = f32[]{:T(128)} all-reduce(f32[]{:T(128)} %multiply_reduce_fusion), channel_id=1, replica_groups=mesh['pipe'=4,'dp'=32] {'dp'}, use_global_device_ids=true, to_apply=%region_88.90 | all-reduce | flops 1 | bytes 8 | tf_op jit(solution)/shard_map/psum | solution.py:218
  (587 shorter events, 631.7 us)
Async XLA Ops:
  7.2 79.4 %all-gather.3.cloned.1.call-start = ((), (), s32[]{:S(2)}) async-start(), calls=%async_computation.2 | async-start | bytes 17301504 | tf_op jit(solution)/shard_map/all_gather | solution.py:107
  7.9 1436.9 %reduce-scatter.2.cloned.1.call-start = ((), (), s32[]{:S(2)}) async-start(), calls=%async_computation.1 | async-start | bytes 17301504 | tf_op jit(solution)/shard_map/reduce_scatter | solution.py:189
  86.6 0.7 copy-start.1
  92.1 3.6 copy-start.5
  168.1 2.8 copy-start
  172.0 0.7 copy-start.11
  172.7 7.4 collective-permute-start
  181.9 5.9 copy-start.6
  263.6 9.2 collective-permute-start.1
  274.3 5.9 copy-start.7
  355.9 8.3 collective-permute-start.2
  365.7 6.1 copy-start.8
  447.6 7.6 collective-permute-start.3
  455.2 90.5 %copy-start.4 = (s32[1,64,32]{1,2,0:T(8,128)S(1)}, s32[1,64,32]{1,2,0:T(8,128)}, u32[]{:S(2)}) copy-start(s32[1,64,32]{1,2,0:T(8,128)} %param.113) | copy-start | bytes 24580
  456.2 89.5 %collective-permute-start.4 = (bf16[32,4096]{1,0:T(8,128)(2,1)}, bf16[32,4096]{1,0:T(8,128)(2,1)S(1)}, u32[]{:S(2)}, u32[]{:S(2)}) collective-permute-start(bf16[32,4096]{1,0:T(8,128)(2,1)} %get-tuple-element.1129), channel_id=1, source_target_pairs={{0,32},{32,64},{64,96},{1,33},{33,65},{65,97},{2,34},{34,66},{66,9... | collective-permute-start | bytes 786440 | tf_op jit(solution)/shard_map/ppermute | solution.py:14
  546.9 365.0 %collective-permute-start.5 = (bf16[32,4096]{1,0:T(8,128)(2,1)}, bf16[32,4096]{1,0:T(8,128)(2,1)S(1)}, u32[]{:S(2)}, u32[]{:S(2)}) collective-permute-start(bf16[32,4096]{1,0:T(8,128)(2,1)} %get-tuple-element.1133), channel_id=1, source_target_pairs={{0,32},{32,64},{64,96},{1,33},{33,65},{65,97},{2,34},{34,66},{66,9... | collective-permute-start | bytes 786440 | tf_op jit(solution)/shard_map/ppermute | solution.py:14
  911.9 1.0 copy-start.2
  914.1 84.6 %collective-permute-start.6 = (bf16[32,4096]{1,0:T(8,128)(2,1)S(1)}, bf16[32,4096]{1,0:T(8,128)(2,1)S(1)}, u32[]{:S(2)}, u32[]{:S(2)}) collective-permute-start(bf16[32,4096]{1,0:T(8,128)(2,1)S(1)} %get-tuple-element.1138), channel_id=1, source_target_pairs={{32,0},{64,32},{96,64},{33,1},{65,33},{97,65},{34,2},{66,34},{98,6... | collective-permute-start | bytes 786440 | tf_op jit(solution)/shard_map/ppermute | solution.py:14
  998.8 7.5 collective-permute-start.7
  1006.4 143.5 %collective-permute-start.8 = (bf16[32,4096]{1,0:T(8,128)(2,1)S(1)}, bf16[32,4096]{1,0:T(8,128)(2,1)S(1)}, u32[]{:S(2)}, u32[]{:S(2)}) collective-permute-start(bf16[32,4096]{1,0:T(8,128)(2,1)S(1)} %get-tuple-element.1142), channel_id=1, source_target_pairs={{32,0},{64,32},{96,64},{33,1},{65,33},{97,65},{34,2},{66,34},{98,6... | collective-permute-start | bytes 786440 | tf_op jit(solution)/shard_map/ppermute | solution.py:14
  1170.2 7.1 collective-permute-start.9
  1197.6 7.1 collective-permute-start.10
  1225.7 7.4 collective-permute-start.11
  1324.2 120.6 %copy-start.3 = (bf16[1,2,64,2048]{3,2,1,0:T(8,128)(2,1)S(1)}, bf16[1,2,64,2048]{3,2,1,0:T(8,128)(2,1)}, u32[]{:S(2)}) copy-start(bf16[1,2,64,2048]{3,2,1,0:T(8,128)(2,1)} %param.112) | copy-start | bytes 1572868
  1324.2 120.6 %copy-start.10 = (f32[1,2,64,2048]{3,2,1,0:T(8,128)S(1)}, f32[1,2,64,2048]{3,2,1,0:T(8,128)}, u32[]{:S(2)}) copy-start(f32[1,2,64,2048]{3,2,1,0:T(8,128)} %param.115) | copy-start | bytes 3145732
Sparse Core Ops, SparseCore 0:
  10.3 76.2 all-gather.2
  1324.3 120.4 reduce-scatter.1
where the time goes:
time: 1600 us; the launch traced here: 1590 us
  local copies, waits for them, and re-layouts  494 us (31%)
  waiting for transfers between devices  462 us (29%)
  matrix products  265 us (17%)
  blocking collectives  128 us (8%)
  starting transfers between devices  116 us (7%)
  other arithmetic  103 us (6%)
    ppermute x12, waiting for transfers between devices, shifted(): lax.ppermute(value, axis, [(source, source + steps) for source in range(l...  262 us
    reduce_scatter x1, waiting for transfers between devices, local(): lax.psum_scatter(lax.map(grad_per_group, (index_part, grad_part)).reshape...  120 us
    ppermute x12, starting transfers between devices, shifted(): lax.ppermute(value, axis, [(source, source + steps) for source in range(l...  116 us
    dot_general x32, matrix products, column_per_group(): jnp.einsum('tjk,jbk->tjb', picked, weight_part, preferred_element_type=jn...  110 us
    broadcast_in_dim x8, local copies, waits for them, and re-layouts, dense_transposed(): lax.map(dense_per_group, (section_weights.reshape(group_count, column_gro...  96.3 us
    convert_element_type x8, local copies, waits for them, and re-layouts, dense_per_group(): slab.astype(jnp.bfloat16).reshape(column_group * block_size, features)  95.6 us
    all_gather x1, waiting for transfers between devices, local(): section_weights = lax.all_gather(weights[0], 'dp', axis=0, tiled=True)  78.6 us
    reshape x32, local copies, waits for them, and re-layouts, column_per_group(): jnp.take(normed_blocks, index_part.reshape(-1), axis=1)  78 us
  transfers between devices with their start and end apart: 14, of which 13 were waited for; matrix products, arithmetic and copies ran while one was open for 23% of the time, Pallas kernels for 0%

commit v1 on v0

--- a/solution.py
+++ b/solution.py
@@ -104,7 +104,9 @@
     own_columns = weights.shape[1]
     block_size = weights.shape[2]
     live_index = live_rows[0]
-    section_weights = lax.all_gather(weights[0], "dp", axis=0, tiled=True)
+    section_weights = jnp.concatenate(
+        lax.all_to_all(jnp.stack([weights[0]] * lax.axis_size("dp")), "dp", 0, 0), axis=0
+    )
     tick_count = micro_count + sections - 1
     incoming = jnp.zeros((tokens, features), jnp.bfloat16)
     saved_in = jnp.zeros((micro_count, tokens, features), jnp.bfloat16)

time: 1600 us -> 1750 us (1.094)
  waiting for transfers between devices: 462 us -> 592 us
    all_to_all x0 -> x1, waiting for transfers between devices: none -> 202 us  [local(): lax.all_to_all(jnp.stack([weights[0]] * lax.axis_size('dp')), 'dp', 0, 0)]
    all_gather x1 -> x0, waiting for transfers between devices: 78.6 us -> none  [local(): section_weights = lax.all_gather(weights[0], 'dp', axis=0, tiled=True)]
  transfers between devices with their start and end apart: 14 -> 14, of which waited for: 13 -> 13; matrix products, arithmetic and copies ran while one was open for 23% -> 21% of each run, Pallas kernels for 0% -> 0%
where the time goes in v1:
time: 1750 us; the launch traced here: 1730 us
  waiting for transfers between devices  592 us (34%)
  local copies, waits for them, and re-layouts  500 us (29%)
  matrix products  265 us (15%)
  blocking collectives  128 us (7%)
  starting transfers between devices  125 us (7%)
  other arithmetic  103 us (6%)
    ppermute x12, waiting for transfers between devices, shifted(): lax.ppermute(value, axis, [(source, source + steps) for source in range(l...  257 us
    all_to_all x1, waiting for transfers between devices, local(): lax.all_to_all(jnp.stack([weights[0]] * lax.axis_size('dp')), 'dp', 0, 0)  202 us
    reduce_scatter x1, waiting for transfers between devices, local(): lax.psum_scatter(lax.map(grad_per_group, (index_part, grad_part)).reshape...  133 us
    ppermute x12, starting transfers between devices, shifted(): lax.ppermute(value, axis, [(source, source + steps) for source in range(l...  115 us
    dot_general x32, matrix products, column_per_group(): jnp.einsum('tjk,jbk->tjb', picked, weight_part, preferred_element_type=jn...  110 us
    broadcast_in_dim x8, local copies, waits for them, and re-layouts, dense_transposed(): lax.map(dense_per_group, (section_weights.reshape(group_count, column_gro...  96.3 us
    convert_element_type x8, local copies, waits for them, and re-layouts, dense_per_group(): slab.astype(jnp.bfloat16).reshape(column_group * block_size, features)  95.6 us
    reshape x32, local copies, waits for them, and re-layouts, column_per_group(): jnp.take(normed_blocks, index_part.reshape(-1), axis=1)  78 us
  transfers between devices with their start and end apart: 14, of which 13 were waited for; matrix products, arithmetic and copies ran while one was open for 21% of the time, Pallas kernels for 0%

profile of v1, /device:TPU:1, one launch (start us, length us, event | category | flops | bytes accessed | tf_op | source)
XLA Modules:
  0.0 1731.2 jit_solution(6647151823288985188)
XLA Ops:
  14.0 9.6 all-to-all-start
  23.7 201.9 %all-to-all-done = bf16[32,2,64,2048]{3,2,1,0:T(8,128)(2,1)} async-done(((bf16[32,2,64,2048]{3,2,1,0:T(8,128)(2,1)}), bf16[32,2,64,2048]{3,2,1,0:T(8,128)(2,1)}, u32[]{:S(2)}, u32[]{:S(2)}) %all-to-all-start) | async-done | bytes 16777248 | tf_op jit(solution)/shard_map/all_to_all | solution.py:108
  226.3 84.7 %conditional.14 = (bf16[32,4096]{1,0:T(8,128)(2,1)S(1)}, bf16[4,32,4096]{2,1,0:T(8,128)(2,1)}, bf16[4,32,4096]{2,1,0:T(8,128)(2,1)}, f32[4,32,4096]{2,1,0:T(8,128)}) conditional(s32[]{:T(128)} %convert_element_type.242, () %tuple.272, (bf16[4,32,4096]{2,1,0:T(8,128)(2,1)}, pred[32,4096]{1,0:T(8,128)(4,1)S(1)}, bf16[32,4096]{1,0:T(8,128)(2,1)S(1)}, ...), branch_computations={%region_0.1_spmd, %region_1.7_spmd} | conditional | flops 69864752 | bytes 28608244 | solution.py:135
  234.7 69.9 %while.112 = (s32[]{:T(128)}, f32[8,32,8,64]{3,1,2,0:T(8,128)}, bf16[8,8,64,2048]{3,2,1,0:T(8,128)(2,1)}, s32[8,8,32]{2,1,0:T(8,128)S(1)}, bf16[32,64,64]{2,0,1:T(8,128)(2,1)S(1)}, /*index=5*/s32[]{:T(128)}) while((s32[]{:T(128)}, f32[8,32,8,64]{3,1,2,0:T(8,128)}, bf16[8,8,64,2048]{3,2,1,0:T(8,128)(2,1)}, s32[8,8,32]{2,1,0:T(8,128)S(1)}, ...), condition=%wide.region_4.5_spmd, body=%wide.region_3.4_spmd.sunk | while | flops 67636480 | bytes 11680329 | solution.py:35
  316.6 83.5 %conditional.15 = (bf16[32,4096]{1,0:T(8,128)(2,1)}, bf16[4,32,4096]{2,1,0:T(8,128)(2,1)}, bf16[4,32,4096]{2,1,0:T(8,128)(2,1)}, f32[4,32,4096]{2,1,0:T(8,128)}) conditional(s32[]{:T(128)} %convert_element_type.241, (bf16[4,32,4096]{2,1,0:T(8,128)(2,1)}, bf16[4,32,4096]{2,1,0:T(8,128)(2,1)}, f32[4,32,4096]{2,1,0:T(8,128)}) %tuple.274, ...), branch_computations={%region_6.8_spmd, %region_7.13_spmd} | conditional | flops 69864752 | bytes 21268686 | solution.py:135
  324.4 69.8 %while.113 = (s32[]{:T(128)}, f32[8,32,8,64]{3,1,2,0:T(8,128)}, bf16[8,8,64,2048]{3,2,1,0:T(8,128)(2,1)}, s32[8,8,32]{2,1,0:T(8,128)S(1)}, bf16[32,64,64]{2,0,1:T(8,128)(2,1)S(1)}, /*index=5*/s32[]{:T(128)}) while((s32[]{:T(128)}, f32[8,32,8,64]{3,1,2,0:T(8,128)}, bf16[8,8,64,2048]{3,2,1,0:T(8,128)(2,1)}, s32[8,8,32]{2,1,0:T(8,128)S(1)}, ...), condition=%wide.region_10.11_spmd, body=%wide.region_9.10_spmd.sunk | while | flops 67636480 | bytes 11680329 | solution.py:35
  407.4 83.2 %conditional.16 = (bf16[32,4096]{1,0:T(8,128)(2,1)}, bf16[4,32,4096]{2,1,0:T(8,128)(2,1)}, bf16[4,32,4096]{2,1,0:T(8,128)(2,1)}, f32[4,32,4096]{2,1,0:T(8,128)}) conditional(s32[]{:T(128)} %convert_element_type.240, (bf16[4,32,4096]{2,1,0:T(8,128)(2,1)}, bf16[4,32,4096]{2,1,0:T(8,128)(2,1)}, f32[4,32,4096]{2,1,0:T(8,128)}) %tuple.276, ...), branch_computations={%region_12.14_spmd, %region_13.19_spmd} | conditional | flops 69864752 | bytes 21268686 | solution.py:135
  414.9 69.8 %while.114 = (s32[]{:T(128)}, f32[8,32,8,64]{3,1,2,0:T(8,128)}, bf16[8,8,64,2048]{3,2,1,0:T(8,128)(2,1)}, s32[8,8,32]{2,1,0:T(8,128)S(1)}, bf16[32,64,64]{2,0,1:T(8,128)(2,1)S(1)}, /*index=5*/s32[]{:T(128)}) while((s32[]{:T(128)}, f32[8,32,8,64]{3,1,2,0:T(8,128)}, bf16[8,8,64,2048]{3,2,1,0:T(8,128)(2,1)}, s32[8,8,32]{2,1,0:T(8,128)S(1)}, ...), condition=%wide.region_16.17_spmd, body=%wide.region_15.16_spmd.sunk | while | flops 67636480 | bytes 11680329 | solution.py:35
  497.9 83.4 %conditional.17 = (bf16[32,4096]{1,0:T(8,128)(2,1)}, bf16[4,32,4096]{2,1,0:T(8,128)(2,1)}, bf16[4,32,4096]{2,1,0:T(8,128)(2,1)}, f32[4,32,4096]{2,1,0:T(8,128)}) conditional(s32[]{:T(128)} %convert_element_type.239, (bf16[4,32,4096]{2,1,0:T(8,128)(2,1)}, bf16[4,32,4096]{2,1,0:T(8,128)(2,1)}, f32[4,32,4096]{2,1,0:T(8,128)}) %tuple.278, ...), branch_computations={%region_18.20_spmd, %region_19.25_spmd} | conditional | flops 69864752 | bytes 21268686 | solution.py:135
  505.5 69.8 %while.115 = (s32[]{:T(128)}, f32[8,32,8,64]{3,1,2,0:T(8,128)}, bf16[8,8,64,2048]{3,2,1,0:T(8,128)(2,1)}, s32[8,8,32]{2,1,0:T(8,128)S(1)}, bf16[32,64,64]{2,0,1:T(8,128)(2,1)S(1)}, /*index=5*/s32[]{:T(128)}) while((s32[]{:T(128)}, f32[8,32,8,64]{3,1,2,0:T(8,128)}, bf16[8,8,64,2048]{3,2,1,0:T(8,128)(2,1)}, s32[8,8,32]{2,1,0:T(8,128)S(1)}, ...), condition=%wide.region_22.23_spmd, body=%wide.region_21.22_spmd.sunk | while | flops 67636480 | bytes 11680329 | solution.py:35
  589.5 85.9 %collective-permute-start.4 = (bf16[32,4096]{1,0:T(8,128)(2,1)}, bf16[32,4096]{1,0:T(8,128)(2,1)S(1)}, u32[]{:S(2)}, u32[]{:S(2)}) collective-permute-start(bf16[32,4096]{1,0:T(8,128)(2,1)} %get-tuple-element.1129), channel_id=1, source_target_pairs={{0,32},{32,64},{64,96},{1,33},{33,65},{65,97},{2,34},{34,66},{66,9... | collective-permute-start | bytes 786440 | tf_op jit(solution)/shard_map/ppermute | solution.py:14
  680.2 8.3 collective-permute-start.5
  688.5 356.7 %while.120 = (s32[]{:T(128)}, bf16[8,512,4096]{2,1,0:T(8,128)(2,1)}, bf16[8,8,64,2048]{3,2,1,0:T(8,128)(2,1)}, s32[8,8,32]{2,1,0:T(8,128)}, s32[]{:T(128)}) while((s32[]{:T(128)}, bf16[8,512,4096]{2,1,0:T(8,128)(2,1)}, bf16[8,8,64,2048]{3,2,1,0:T(8,128)(2,1)}, s32[8,8,32]{2,1,0:T(8,128)}, s32[]{:T(128)}) %tuple.519), condition=%wide.region_43.45_spmd.clone, body=%wide.region_42.44_spmd.clone.sunk | while | flops 136331264 | bytes 39849540 | solution.py:63
  704.5 11.9 copy.165
  716.4 12.0 broadcast_in_dim.172
  740.8 8.2 convert_bitcast_fusion.2
  749.0 11.9 copy.165
  761.0 12.0 broadcast_in_dim.172
  785.4 8.2 convert_bitcast_fusion.2
  793.6 11.9 copy.165
  805.6 12.0 broadcast_in_dim.172
  830.0 8.2 convert_bitcast_fusion.2
  838.2 11.9 copy.165
  850.2 12.0 broadcast_in_dim.172
  874.6 8.2 convert_bitcast_fusion.2
  882.8 11.9 copy.165
  894.8 12.0 broadcast_in_dim.172
  919.1 8.2 convert_bitcast_fusion.2
  927.3 11.9 copy.165
  939.3 12.0 broadcast_in_dim.172
  963.7 8.2 convert_bitcast_fusion.2
  971.9 11.9 copy.165
  983.9 12.0 broadcast_in_dim.172
  1008.3 8.2 convert_bitcast_fusion.2
  1016.6 11.9 copy.165
  1028.5 12.0 broadcast_in_dim.172
  1048.8 82.4 %collective-permute-done.6 = bf16[32,4096]{1,0:T(8,128)(2,1)S(1)} collective-permute-done((bf16[32,4096]{1,0:T(8,128)(2,1)S(1)}, bf16[32,4096]{1,0:T(8,128)(2,1)S(1)}, u32[]{:S(2)}, u32[]{:S(2)}) %collective-permute-start.6) | collective-permute-done | bytes 262176 | tf_op jit(solution)/shard_map/ppermute | solution.py:14
  1141.0 140.7 %collective-permute-done.8 = bf16[32,4096]{1,0:T(8,128)(2,1)S(1)} collective-permute-done((bf16[32,4096]{1,0:T(8,128)(2,1)S(1)}, bf16[32,4096]{1,0:T(8,128)(2,1)S(1)}, u32[]{:S(2)}, u32[]{:S(2)}) %collective-permute-start.8) | collective-permute-done | bytes 262176 | tf_op jit(solution)/shard_map/ppermute | solution.py:14
  1281.7 20.3 %conditional.24 = (bf16[32,4096]{1,0:T(8,128)(2,1)S(1)}, bf16[4,32,4096]{2,1,0:T(8,128)(2,1)}) conditional(s32[]{:T(128)} %convert_element_type.232, bf16[4,32,4096]{2,1,0:T(8,128)(2,1)} %get-tuple-element.1141, (pred[32,4096]{1,0:T(8,128)(4,1)S(1)}, bf16[32,4096]{1,0:T(8,128)(2,1)S(1)}, bf16[32,4096]{1,0:T(8,128)(2,1)S(1)}, s32[]{:T(128)}, ...), branch_computations={%region_59.61_spmd, %region_60.65_spmd} | conditional | flops 1077411840 | bytes 38537416 | solution.py:164
  1286.9 13.9 fusion.45
  1309.1 20.3 %conditional.25 = (bf16[32,4096]{1,0:T(8,128)(2,1)S(1)}, bf16[4,32,4096]{2,1,0:T(8,128)(2,1)}) conditional(s32[]{:T(128)} %convert_element_type.231, bf16[4,32,4096]{2,1,0:T(8,128)(2,1)} %get-tuple-element.1143, (pred[32,4096]{1,0:T(8,128)(4,1)S(1)}, bf16[32,4096]{1,0:T(8,128)(2,1)S(1)}, bf16[32,4096]{1,0:T(8,128)(2,1)S(1)}, s32[]{:T(128)}, ...), branch_computations={%region_64.66_spmd, %region_65.70_spmd} | conditional | flops 1077411840 | bytes 38537416 | solution.py:164
  1314.3 13.9 fusion.59
  1336.5 21.0 %conditional.26 = (bf16[32,4096]{1,0:T(8,128)(2,1)}, bf16[4,32,4096]{2,1,0:T(8,128)(2,1)}) conditional(s32[]{:T(128)} %convert_element_type.230, bf16[4,32,4096]{2,1,0:T(8,128)(2,1)} %get-tuple-element.1145, (pred[32,4096]{1,0:T(8,128)(4,1)S(1)}, bf16[32,4096]{1,0:T(8,128)(2,1)S(1)}, bf16[32,4096]{1,0:T(8,128)(2,1)S(1)}, s32[]{:T(128)}, ...), branch_computations={%region_69.71_spmd, %region_70.75_spmd} | conditional | flops 1077411840 | bytes 38537416 | solution.py:164
  1341.8 13.9 fusion.73
  1375.4 80.6 %while.119 = (s32[]{:T(128)}, bf16[8,8,64,2048]{3,2,1,0:T(8,128)(2,1)}, bf16[8,128,8,64]{1,3,2,0:T(8,128)(2,1)}, s32[8,8,32]{2,1,0:T(8,128)}, bf16[128,64,64]{0,2,1:T(8,128)(2,1)S(1)}, /*index=5*/s32[]{:T(128)}) while((s32[]{:T(128)}, bf16[8,8,64,2048]{3,2,1,0:T(8,128)(2,1)}, bf16[8,128,8,64]{1,3,2,0:T(8,128)(2,1)}, ...), condition=%wide.region_78.80_spmd, body=%wide.region_77.79_spmd.sunk | while | flops 272633088 | bytes 14890569 | solution.py:192
  1456.2 132.6 %reduce-scatter.2.cloned.1.call-done = bf16[2,64,2048]{2,1,0:T(8,128)(2,1)} async-done(((bf16[64,64,2048]{2,1,0:T(8,128)(2,1)}), bf16[2,64,2048]{2,1,0:T(8,128)(2,1)}) %reduce-scatter.2.cloned.1.call-update) | async-done | bytes 524304 | tf_op jit(solution)/shard_map/reduce_scatter | solution.py:191
  1593.1 63.9 %psum.14 = f32[32]{0:T(128)S(1)} all-reduce(f32[32]{0:T(128)S(1)} %select_reduce_fusion.1), channel_id=1, replica_groups=mesh['pipe'=4,'dp'=32] {'dp'}, use_global_device_ids=true, to_apply=%region_85.87 | all-reduce | flops 32 | bytes 256 | tf_op jit(solution)/shard_map/psum | solution.py:217
  1658.3 64.2 %psum.15 = f32[]{:T(128)} all-reduce(f32[]{:T(128)} %multiply_reduce_fusion), channel_id=1, replica_groups=mesh['pipe'=4,'dp'=32] {'dp'}, use_global_device_ids=true, to_apply=%region_88.90 | all-reduce | flops 1 | bytes 8 | tf_op jit(solution)/shard_map/psum | solution.py:220
  (579 shorter events, 639.9 us)
Async XLA Ops:
  14.0 211.6 %copy-start.4 = (s32[1,64,32]{1,2,0:T(8,128)S(1)}, s32[1,64,32]{1,2,0:T(8,128)}, u32[]{:S(2)}) copy-start(s32[1,64,32]{1,2,0:T(8,128)} %param.113) | copy-start | bytes 24580
  14.0 211.6 %all-to-all-start = ((bf16[32,2,64,2048]{3,2,1,0:T(8,128)(2,1)}), bf16[32,2,64,2048]{3,2,1,0:T(8,128)(2,1)}, u32[]{:S(2)}, u32[]{:S(2)}) async-start(bf16[32,2,64,2048]{3,2,1,0:T(8,128)(2,1)} %stack.3), calls=%async_computation | async-start | bytes 33554432 | tf_op jit(solution)/shard_map/all_to_all | solution.py:108
  23.6 1565.2 %reduce-scatter.2.cloned.1.call-start = ((), (), s32[]{:S(2)}) async-start(), calls=%async_computation.2 | async-start | bytes 17301504 | tf_op jit(solution)/shard_map/reduce_scatter | solution.py:191
  225.6 0.7 copy-start.1
  307.1 2.8 copy-start
  311.0 0.7 copy-start.6
  311.7 4.9 collective-permute-start
  400.1 7.3 collective-permute-start.1
  490.5 7.3 collective-permute-start.2
  581.3 7.3 collective-permute-start.3
  589.5 89.5 %collective-permute-start.4 = (bf16[32,4096]{1,0:T(8,128)(2,1)}, bf16[32,4096]{1,0:T(8,128)(2,1)S(1)}, u32[]{:S(2)}, u32[]{:S(2)}) collective-permute-start(bf16[32,4096]{1,0:T(8,128)(2,1)} %get-tuple-element.1129), channel_id=1, source_target_pairs={{0,32},{32,64},{64,96},{1,33},{33,65},{65,97},{2,34},{34,66},{66,9... | collective-permute-start | bytes 786440 | tf_op jit(solution)/shard_map/ppermute | solution.py:14
  680.2 365.0 %collective-permute-start.5 = (bf16[32,4096]{1,0:T(8,128)(2,1)}, bf16[32,4096]{1,0:T(8,128)(2,1)S(1)}, u32[]{:S(2)}, u32[]{:S(2)}) collective-permute-start(bf16[32,4096]{1,0:T(8,128)(2,1)} %get-tuple-element.1133), channel_id=1, source_target_pairs={{0,32},{32,64},{64,96},{1,33},{33,65},{65,97},{2,34},{34,66},{66,9... | collective-permute-start | bytes 786440 | tf_op jit(solution)/shard_map/ppermute | solution.py:14
  1045.2 1.0 copy-start.2
  1047.5 83.7 %collective-permute-start.6 = (bf16[32,4096]{1,0:T(8,128)(2,1)S(1)}, bf16[32,4096]{1,0:T(8,128)(2,1)S(1)}, u32[]{:S(2)}, u32[]{:S(2)}) collective-permute-start(bf16[32,4096]{1,0:T(8,128)(2,1)S(1)} %get-tuple-element.1138), channel_id=1, source_target_pairs={{32,0},{64,32},{96,64},{33,1},{65,33},{97,65},{34,2},{66,34},{98,6... | collective-permute-start | bytes 786440 | tf_op jit(solution)/shard_map/ppermute | solution.py:14
  1131.2 7.1 collective-permute-start.7
  1138.3 143.4 %collective-permute-start.8 = (bf16[32,4096]{1,0:T(8,128)(2,1)S(1)}, bf16[32,4096]{1,0:T(8,128)(2,1)S(1)}, u32[]{:S(2)}, u32[]{:S(2)}) collective-permute-start(bf16[32,4096]{1,0:T(8,128)(2,1)S(1)} %get-tuple-element.1142), channel_id=1, source_target_pairs={{32,0},{64,32},{96,64},{33,1},{65,33},{97,65},{34,2},{66,34},{98,6... | collective-permute-start | bytes 786440 | tf_op jit(solution)/shard_map/ppermute | solution.py:14
  1302.0 7.1 collective-permute-start.9
  1329.4 7.1 collective-permute-start.10
  1357.5 7.4 collective-permute-start.11
  1456.0 132.8 %copy-start.3 = (bf16[1,2,64,2048]{3,2,1,0:T(8,128)(2,1)S(1)}, bf16[1,2,64,2048]{3,2,1,0:T(8,128)(2,1)}, u32[]{:S(2)}) copy-start(bf16[1,2,64,2048]{3,2,1,0:T(8,128)(2,1)} %param.112) | copy-start | bytes 1572868
  1456.0 132.8 %copy-start.5 = (f32[1,2,64,2048]{3,2,1,0:T(8,128)S(1)}, f32[1,2,64,2048]{3,2,1,0:T(8,128)}, u32[]{:S(2)}) copy-start(f32[1,2,64,2048]{3,2,1,0:T(8,128)} %param.115) | copy-start | bytes 3145732
Sparse Core Ops, SparseCore 0:
  1456.1 132.6 reduce-scatter.1
